TPU v7x, 256 devices: a whole 4x4x8 slice. The times are simulated.
256 devices in a mesh: lane: 64 (over y_hi, x, z), group: 4 (over y_lo, core).
Axes of the slice: x: 4, y: 4 (y_hi: 2, y_lo: 2; y = y_hi * 2 + y_lo), z: 8, core: 2. Of those that a mesh axis runs over, the one named last changes fastest.
Arguments:
- half_vectors: bfloat16 [2048, 768, 512], P('lane', None, 'group'), may hold values from -2.5 to 2.5
- mo_coeff: bfloat16 [768, 512], replicated, may hold values from -0.21875 to 0.21875
- amplitudes: bfloat16 [512, 4, 128, 512], P('group', None, 'lane'), may hold values from -0.01171875 to 0.01171875
Outputs:
- ladder: float32 [512, 4, 512], P('lane', None, 'group')
All inputs are finite; a program needn't handle non-finite values.
Results may differ from a plain program's by a relative error of at most 0.0049.
Values may be sent and summed in bfloat16 or wider, within the bound.
No kernel may reach another device: no remote copies, remote signals or barrier semaphores. Data moves between devices by JAX's collectives and lax.ppermute only.
A program may use at most 128 MiB of HBM per device.

v0:
```python
import jax
import jax.numpy as jnp
from jax import lax
from jax.experimental import pallas as pl
from jax.experimental.pallas import tpu as pltpu
from jax.sharding import Mesh, PartitionSpec as P


AROWS = 4
LANE = ("yh", "x", "z")
GROUP = ("yl", "co")
EVERY = LANE + GROUP
PHASES = 2
Z_STEPS = (1, 2, 7)
Z_OFF = (0, 1, 2, 3, 7, 6, 5, 4)
SIZES = {"yh": 2, "x": 4, "z": 8, "yl": 2, "co": 2}


def swap(block, axis, flip):
    count = 4 if isinstance(axis, tuple) else SIZES[axis]
    return lax.ppermute(block, axis, [(i, i ^ flip) for i in range(count)])


def double(block, axis, flip):
    return jnp.concatenate([block, swap(block, axis, flip)], axis=0)


def vec_kernel(half_ref, mo_ref, *refs):
    send_ref, rows = refs[-2:]
    part, _, nc = half_ref.shape
    lanes, groups, dl, step, nb = send_ref.shape
    now = pl.program_id(0)

    @pl.when(now < PHASES)
    def _():
        for i in range(part):
            full = lax.dot_general(
                half_ref[i], mo_ref[...], (((0,), (0,)), ((), ())),
                preferred_element_type=jnp.float32,
            )
            row = pl.multiple_of((now * part + i) * nc, nc)
            for g in range(groups):
                rows[g, pl.ds(row, nc), :] = full[:, g * nb : (g + 1) * nb]

    @pl.when(now >= PHASES)
    def _():
        first = (now - PHASES) * lanes * dl

        @pl.loop(0, lanes, unroll=8)
        def _(lane):
            for j in range(dl):
                for g in range(groups):
                    piece = rows[g, pl.ds(first + lane * dl + j, step, stride=nc), :]
                    send_ref[lane, g, j] = piece.astype(send_ref.dtype)


def make_vec(half, mo, lanes, groups, which, send=None):
    nl, nao, nc = half.shape
    nv = mo.shape[1]
    dl, nb = nc // lanes, nv // groups
    step = nl // 2
    ins = [
        pl.BlockSpec(
            (step // PHASES, nao, nc),
            lambda i: (which * PHASES + jnp.minimum(i, PHASES - 1), 0, 0),
        ),
        pl.BlockSpec((nao, nv), lambda i: (0, 0)),
    ]
    args = (half, mo)
    if send is not None:
        ins.append(pl.BlockSpec(memory_space=pl.ANY))
        args += (send,)
    return pl.pallas_call(
        vec_kernel,
        grid=(2 * PHASES,),
        in_specs=ins,
        out_specs=pl.BlockSpec(
            (lanes // PHASES, groups, dl, step, nb),
            lambda i: (jnp.maximum(i - PHASES, 0), 0, 0, which, 0),
        ),
        out_shape=jax.ShapeDtypeStruct((lanes, groups, dl, nl, nb), jnp.bfloat16),
        scratch_shapes=[pltpu.VMEM((groups, step * nc, nb), jnp.float32)],
        input_output_aliases={2: 0} if send is not None else {},
        cost_estimate=pl.CostEstimate(
            flops=2 * step * nao * nc * nv,
            transcendentals=0,
            bytes_accessed=2 * step * (nao * nc + nc * nv),
        ),
        name="vec",
    )(*args)


def ladder_kernel(where_ref, got_hbm, *refs):
    turned, panels, total, got_sem, side_sem = refs[-5:]
    count = side_sem.shape[0]
    side_hbm, out_ref, got_ref, sides = refs[:count], refs[count], refs[count + 1], refs[count + 2 : -5]
    nyh, nx, nz, nyl, nco, dl, nl, nb = got_ref.shape
    nd = nyl * nco * dl
    nc, npair = sides[-1].shape[-2:]
    run = nz * nl
    at_yh, at_x, at_z = where_ref[0], where_ref[1], where_ref[2]

    def got_copy(sy, sx):
        at = (at_yh ^ sy, at_x ^ sx)
        return pltpu.make_async_copy(got_hbm.at[at], got_ref.at[sy, sx], got_sem.at[sy, sx])

    def side_copy(i, half):
        source = 1 - half if i < count - nco and i % nyh else half
        return pltpu.make_async_copy(
            side_hbm[i].at[source], sides[i].at[half], side_sem.at[i, half]
        )

    order = [(sx, sy) for sx in range(nx) for sy in range(nyh)]
    for sx, sy in order:
        got_copy(sy, sx).start()
    total[...] = jnp.zeros_like(total)

    for k, (sx, sy) in enumerate(order):
        got_copy(sy, sx).wait()
        if k == 0:
            for i in range(count):
                side_copy(i, 0).start()
        for d in range(nd):
            yl, co, j = d // (nco * dl), d // dl % nco, d % dl
            parts = [got_ref[sy, sx, at_z ^ Z_OFF[sz], yl, co, j] for sz in range(nz)]
            turned[d * nb : (d + 1) * nb, k * run : (k + 1) * run] = jnp.transpose(
                jnp.concatenate(parts, axis=0)
            )

    @pl.loop(0, nyl)
    def _(half):
        for i in range(count - nco):
            side_copy(i, half).wait()

        @pl.when(half + 1 < nyl)
        def _():
            for i in range(count):
                side_copy(i, half + 1).start()

        @pl.loop(0, AROWS)
        def _(arow):
            weights = jnp.concatenate(
                [
                    jnp.concatenate(
                        [piece[half, :, arow].reshape(-1, nc) for piece in pieces], axis=0
                    )
                    for pieces in (sides[: count // 2 - 1], sides[count // 2 - 1 : -2])
                ],
                axis=1,
            )
            panel = jnp.dot(turned[...], weights, preferred_element_type=jnp.float32)
            panel = panel.astype(jnp.bfloat16)
            row = pl.multiple_of(arow * nb, nb)
            for co in range(nco):
                for d in range(nd):
                    panels[pl.ds(row, nb), (co * nd + d) * nc : (co * nd + d + 1) * nc] = panel[
                        d * nb : (d + 1) * nb, co * nc : (co + 1) * nc
                    ]

        for i in range(count - nco, count):
            side_copy(i, half).wait()
        for co in range(nco):
            total[...] += jnp.dot(
                panels[:, co * nd * nc : (co + 1) * nd * nc],
                sides[count - nco + co][half].reshape(nd * nc, npair),
                preferred_element_type=jnp.float32,
            )

    out_ref[...] = jnp.transpose(total[...].astype(jnp.bfloat16))


def make_ladder(where, got, pairs, amps):
    nyh, nx, nz, nyl, nco, _, nl, nb = got.shape
    nd, nc, npair = amps[0].shape[1:]
    deep = nyh * nx * nz * nl
    sides = list(pairs) + list(amps)
    return pl.pallas_call(
        ladder_kernel,
        in_specs=[pl.BlockSpec(memory_space=pltpu.SMEM)]
        + [pl.BlockSpec(memory_space=pl.ANY)] * (1 + len(sides)),
        out_specs=pl.BlockSpec(memory_space=pltpu.VMEM),
        scratch_shapes=[pltpu.VMEM(side.shape, side.dtype) for side in [got] + sides]
        + [
            pltpu.VMEM((nd * nb, deep), jnp.bfloat16),
            pltpu.VMEM((AROWS * nb, nco * nd * nc), jnp.bfloat16),
            pltpu.VMEM((AROWS * nb, npair), jnp.float32),
            pltpu.SemaphoreType.DMA((nyh, nx)),
            pltpu.SemaphoreType.DMA((len(sides), nyl)),
        ],
        out_shape=jax.ShapeDtypeStruct((npair, AROWS * nb), jnp.bfloat16),
        compiler_params=pltpu.CompilerParams(vmem_limit_bytes=34 << 20),
        name="ladder",
    )(where, got, *sides)


def body(half, mo, amp):
    nl, _, nc = half.shape
    nv = mo.shape[1]
    npair = amp.shape[3]
    lanes = SIZES["yh"] * SIZES["x"] * SIZES["z"]
    groups = SIZES["yl"] * SIZES["co"]
    dl, nb = nc // lanes, nv // groups

    pair = jnp.einsum("lmc,ma->alc", half, mo[:, :AROWS], preferred_element_type=jnp.float32)
    pair = pair.astype(jnp.bfloat16)[None]
    half, pair, amp = lax.optimization_barrier((half, pair, amp))
    amp = jnp.transpose(amp.reshape(nc, groups * dl, npair), (1, 0, 2))[None]
    amp_far = swap(amp, "yl", 1)
    send = make_vec(half, mo, lanes, groups, 0)
    pair = double(pair, "z", Z_STEPS[0])
    send, pair = lax.optimization_barrier((send, pair))
    send = make_vec(half, mo, lanes, groups, 1, send)
    pair = double(pair, "z", Z_STEPS[1])
    pair = double(pair, "z", Z_STEPS[2])
    send, pair = lax.optimization_barrier((send, pair))
    send = send.reshape(lanes * groups, dl * nl, nb)
    got = lax.all_to_all(send, EVERY, 0, 0, tiled=True)
    got = got.reshape(2, 4, 8, 2, 2, dl, nl, nb)
    pair = pair[None]
    near = swap(pair, ("yh", "yl"), 1)
    same = [jnp.concatenate([pair, near], axis=0), None]
    same[1] = swap(same[0], ("yh", "yl"), 3)
    one = [swap(same[0], "x", 1), None]
    three = [swap(same[0], "x", 3), None]
    one[1] = swap(same[1], "x", 1)
    three[1] = swap(same[1], "x", 3)
    two = [swap(three[0], "x", 1), swap(one[1], "x", 3)]
    pieces = same + one + two + three
    pairs = pieces + [swap(piece, "co", 1) for piece in pieces]
    amp = jnp.concatenate([amp, amp_far], axis=0)
    amps = [amp, swap(amp, "co", 1)]

    where = jnp.stack([lax.axis_index("yh"), lax.axis_index("x"), lax.axis_index("z")])
    part = make_ladder(where.astype(jnp.int32), got, pairs, amps)
    part = lax.all_to_all(
        part.reshape(lanes, npair // lanes, AROWS * nb), LANE, 0, 0, tiled=True
    )
    part = jnp.sum(part.astype(jnp.float32), axis=0)
    return part.reshape(npair // lanes, AROWS, nb)


def solution(mesh):
    fine = Mesh(mesh.devices.reshape(tuple(SIZES.values())), EVERY)
    in_specs = (P(LANE, None, GROUP), P(), P(GROUP, None, LANE, None))
    out_specs = P(LANE, None, GROUP)
    return jax.shard_map(
        body, mesh=fine, in_specs=in_specs, out_specs=out_specs, check_vma=False
    )
```

profile of v0, /device:TPU:0, one launch (start us, length us, event | category | flops | bytes accessed | tf_op | source)
XLA Modules:
  0.0 225.9 jit_solution(11302614711996952702)
XLA Ops:
  0.0 3.9 %fusion = bf16[4,32,128]{2,0,1:T(4,128)(2,1)S(1)} fusion(bf16[32,768,128]{2,1,0:T(8,128)(2,1)} %half_ref.1, bf16[768,512]{1,0:T(8,128)(2,1)} %mo_ref.3), kind=kOutput, calls=%fused_computation.4 | convolution fusion | flops 25165824 | bytes 6520832 | tf_op jit(solution)/shard_map/lmc,ma->alc/dot_general | solution.py:204
  4.2 7.3 %vec.2.refs_0_ = bf16[64,4,2,32,128]{4,3,2,1,0:T(8,128)(2,1)} custom-call(bf16[32,768,128]{2,1,0:T(8,128)(2,1)} %half_ref.1, bf16[768,512]{1,0:T(8,128)(2,1)} %mo_ref.3), custom_call_target="tpu_custom_call" | custom-call | flops 1610612736 | bytes 5242880 | tf_op jit(solution)/shard_map/vec/pallas_call | solution.py:73
  11.5 3.4 %collective-permute-start.1 = (bf16[2,4,32,128]{3,2,1,0:T(8,128)(2,1)S(1)}, bf16[2,4,32,128]{3,2,1,0:T(8,128)(2,1)S(1)}, u32[]{:S(2)}, u32[]{:S(2)}) collective-permute-start(bf16[2,4,32,128]{3,2,1,0:T(8,128)(2,1)S(1)} %pad_maximum_fusion.4), channel_id=1, source_target_pairs={{0,8},{4,12},{8,0},{12,4},{16,24},{20,28},{24,16},{28,20},{1,9},{5... | collective-permute-start | bytes 196616 | tf_op jit(solution)/shard_map/ppermute | solution.py:21
  14.8 2.3 %collective-permute-done.1 = bf16[2,4,32,128]{3,2,1,0:T(8,128)(2,1)S(1)} collective-permute-done((bf16[2,4,32,128]{3,2,1,0:T(8,128)(2,1)S(1)}, bf16[2,4,32,128]{3,2,1,0:T(8,128)(2,1)S(1)}, u32[]{:S(2)}, u32[]{:S(2)}) %collective-permute-start.1) | collective-permute-done | bytes 65568 | tf_op jit(solution)/shard_map/ppermute | solution.py:21
  17.1 5.5 %collective-permute-start.2 = (bf16[4,4,32,128]{3,2,1,0:T(8,128)(2,1)S(1)}, bf16[4,4,32,128]{3,2,1,0:T(8,128)(2,1)S(1)}, u32[]{:S(2)}, u32[]{:S(2)}) collective-permute-start(bf16[4,4,32,128]{3,2,1,0:T(8,128)(2,1)S(1)} %pad_maximum_fusion.3), channel_id=1, source_target_pairs={{0,28},{4,24},{8,20},{12,16},{16,12},{20,8},{24,4},{28,0},{1,29},{... | collective-permute-start | bytes 393224 | tf_op jit(solution)/shard_map/ppermute | solution.py:21
  22.6 7.2 %vec.3 = bf16[64,4,2,32,128]{4,3,2,1,0:T(8,128)(2,1)} custom-call(bf16[32,768,128]{2,1,0:T(8,128)(2,1)} %half_ref.1, bf16[768,512]{1,0:T(8,128)(2,1)} %mo_ref.3, bf16[64,4,2,32,128]{4,3,2,1,0:T(8,128)(2,1)} %vec.2.refs_0_), custom_call_target="tpu_custom_call", output_to_operand_aliasing={{}: (2, {})} | custom-call | flops 1610612736 | bytes 5242880 | tf_op jit(solution)/shard_map/vec/pallas_call | solution.py:73
  29.9 12.0 %all-to-all-start = ((bf16[256,64,128]{2,1,0:T(8,128)(2,1)}), bf16[256,64,128]{2,1,0:T(8,128)(2,1)}, u32[]{:S(2)}, u32[]{:S(2)}) async-start(bf16[256,64,128]{2,1,0:T(8,128)(2,1)} %bitcast.21), calls=%async_computation | async-start | bytes 8388608 | tf_op jit(solution)/shard_map/all_to_all | solution.py:217
  42.3 2.0 collective-permute-start.3
  44.3 54.0 %collective-permute-done.3 = bf16[1,8,4,32,128]{4,3,2,1,0:T(8,128)(2,1)S(1)} collective-permute-done((bf16[1,8,4,32,128]{4,3,2,1,0:T(8,128)(2,1)S(1)}, bf16[1,8,4,32,128]{4,3,2,1,0:T(8,128)(2,1)S(1)}, u32[]{:S(2)}, u32[]{:S(2)}) %collective-permute-start.3) | collective-permute-done | bytes 262176 | tf_op jit(solution)/shard_map/ppermute | solution.py:21
  98.5 3.1 %collective-permute-start.7 = (bf16[2,8,4,32,128]{4,3,2,1,0:T(8,128)(2,1)S(1)}, bf16[2,8,4,32,128]{4,3,2,1,0:T(8,128)(2,1)S(1)}, u32[]{:S(2)}, u32[]{:S(2)}) collective-permute-start(bf16[2,8,4,32,128]{4,3,2,1,0:T(8,128)(2,1)S(1)} %pad_maximum_fusion.1.refs_0_), channel_id=1, source_target_pairs={{0,96},{32,64},{64,32},{96,0},{1,97},{33,65},{65,33},{97,1},{2,98}... | collective-permute-start | bytes 1572872 | tf_op jit(solution)/shard_map/ppermute | solution.py:21
  101.6 2.1 collective-permute-start.4
  104.1 19.2 %collective-permute-done.7.refs_6_ = bf16[2,8,4,32,128]{4,3,2,1,0:T(8,128)(2,1)S(1)} collective-permute-done((bf16[2,8,4,32,128]{4,3,2,1,0:T(8,128)(2,1)S(1)}, bf16[2,8,4,32,128]{4,3,2,1,0:T(8,128)(2,1)S(1)}, u32[]{:S(2)}, u32[]{:S(2)}) %collective-permute-start.7) | collective-permute-done | bytes 524320 | tf_op jit(solution)/shard_map/ppermute | solution.py:21
  125.1 1.2 collective-permute-start.6
  129.3 12.0 %collective-permute-done.8.refs_4_ = bf16[2,8,4,32,128]{4,3,2,1,0:T(8,128)(2,1)} collective-permute-done((bf16[2,8,4,32,128]{4,3,2,1,0:T(8,128)(2,1)S(1)}, bf16[2,8,4,32,128]{4,3,2,1,0:T(8,128)(2,1)}, u32[]{:S(2)}, u32[]{:S(2)}) %collective-permute-start.8) | collective-permute-done | bytes 524320 | tf_op jit(solution)/shard_map/ppermute | solution.py:21
  142.5 10.0 %collective-permute-done.6.refs_3_ = bf16[2,8,4,32,128]{4,3,2,1,0:T(8,128)(2,1)} collective-permute-done((bf16[2,8,4,32,128]{4,3,2,1,0:T(8,128)(2,1)S(1)}, bf16[2,8,4,32,128]{4,3,2,1,0:T(8,128)(2,1)}, u32[]{:S(2)}, u32[]{:S(2)}) %collective-permute-start.6) | collective-permute-done | bytes 524320 | tf_op jit(solution)/shard_map/ppermute | solution.py:21
  154.7 1.7 collective-permute-done.10.refs_7_
  156.4 11.4 %collective-permute-done.9.refs_5_ = bf16[2,8,4,32,128]{4,3,2,1,0:T(8,128)(2,1)} collective-permute-done((bf16[2,8,4,32,128]{4,3,2,1,0:T(8,128)(2,1)}, bf16[2,8,4,32,128]{4,3,2,1,0:T(8,128)(2,1)}, u32[]{:S(2)}, u32[]{:S(2)}) %collective-permute-start.9) | collective-permute-done | bytes 524320 | tf_op jit(solution)/shard_map/ppermute | solution.py:21
  168.0 2.2 collective-permute-done.16.refs_13_
  171.2 1.0 copy-done.3
  172.2 1.0 copy-done.5
  173.3 1.0 copy-done.7
  175.3 1.0 copy-done.11
  176.4 16.9 %ladder.1 = bf16[512,512]{1,0:T(8,128)(2,1)S(1)} custom-call(s32[3]{0:T(128)S(1)} %pad_add_fusion.where_ref, bf16[2,4,8,2,2,2,32,128]{7,6,5,4,3,2,1,0:T(8,128)(2,1)} %bitcast.6.got_hbm, bf16[2,8,4,32,128]{4,3,2,1,0:T(8,128)(2,1)S(1)} %pad_maximum_fusion.1.refs_0_, bf16[2,8,4,32,128]{4,3,2,1,0:T(8,128)(2,1)S(1)} %copy-done.3, ...), custom_call_target="tpu_custom_call" | custom-call | tf_op jit(solution)/shard_map/ladder/pallas_call | solution.py:177
  193.3 31.9 %all_to_all.10 = bf16[64,8,512]{2,1,0:T(8,128)(2,1)S(1)} all-to-all(bf16[64,8,512]{2,1,0:T(8,128)(2,1)S(1)} %bitcast.20), channel_id=1, replica_groups=mesh['yh'=2,'x'=4,'z'=8,'yl'=2,'co'=2] {'yh','x','z'}, dimensions={0} | all-to-all | bytes 1048576 | tf_op jit(solution)/shard_map/all_to_all | solution.py:235
  (61 shorter events, 12.3 us)
Async XLA Ops:
  3.9 7.6 %collective-permute-start = (bf16[1,4,32,128]{3,2,1,0:T(8,128)(2,1)S(1)}, bf16[1,4,32,128]{3,2,1,0:T(8,128)(2,1)S(1)}, u32[]{:S(2)}, u32[]{:S(2)}) collective-permute-start(bf16[1,4,32,128]{3,2,1,0:T(8,128)(2,1)S(1)} %bitcast.26), channel_id=1, source_target_pairs={{0,4},{4,0},{8,12},{12,8},{16,20},{20,16},{24,28},{28,24},{1,5},{5... | collective-permute-start | bytes 98312 | tf_op jit(solution)/shard_map/ppermute | solution.py:21
  11.5 5.6 %collective-permute-start.1 = (bf16[2,4,32,128]{3,2,1,0:T(8,128)(2,1)S(1)}, bf16[2,4,32,128]{3,2,1,0:T(8,128)(2,1)S(1)}, u32[]{:S(2)}, u32[]{:S(2)}) collective-permute-start(bf16[2,4,32,128]{3,2,1,0:T(8,128)(2,1)S(1)} %pad_maximum_fusion.4), channel_id=1, source_target_pairs={{0,8},{4,12},{8,0},{12,4},{16,24},{20,28},{24,16},{28,20},{1,9},{5... | collective-permute-start | bytes 196616 | tf_op jit(solution)/shard_map/ppermute | solution.py:21
  17.1 12.7 %collective-permute-start.2 = (bf16[4,4,32,128]{3,2,1,0:T(8,128)(2,1)S(1)}, bf16[4,4,32,128]{3,2,1,0:T(8,128)(2,1)S(1)}, u32[]{:S(2)}, u32[]{:S(2)}) collective-permute-start(bf16[4,4,32,128]{3,2,1,0:T(8,128)(2,1)S(1)} %pad_maximum_fusion.3), channel_id=1, source_target_pairs={{0,28},{4,24},{8,20},{12,16},{16,12},{20,8},{24,4},{28,0},{1,29},{... | collective-permute-start | bytes 393224 | tf_op jit(solution)/shard_map/ppermute | solution.py:21
  29.9 12.0 %copy-start.12 = (bf16[128,4,2,512]{3,2,1,0:T(2,128)(2,1)S(1)}, bf16[128,4,2,512]{3,2,1,0:T(2,128)(2,1)}, u32[]{:S(2)}) copy-start(bf16[128,4,2,512]{3,2,1,0:T(2,128)(2,1)} %param.5) | copy-start | bytes 3145732
  29.9 140.3 %all-to-all-start = ((bf16[256,64,128]{2,1,0:T(8,128)(2,1)}), bf16[256,64,128]{2,1,0:T(8,128)(2,1)}, u32[]{:S(2)}, u32[]{:S(2)}) async-start(bf16[256,64,128]{2,1,0:T(8,128)(2,1)} %bitcast.21), calls=%async_computation | async-start | bytes 8388608 | tf_op jit(solution)/shard_map/all_to_all | solution.py:217
  42.2 61.5 %collective-permute-start.19 = (bf16[1,8,128,512]{3,2,1,0:T(8,128)(2,1)S(1)}, bf16[1,8,128,512]{3,2,1,0:T(8,128)(2,1)S(1)}, u32[]{:S(2)}, u32[]{:S(2)}) collective-permute-start(bf16[1,8,128,512]{3,2,1,0:T(8,128)(2,1)S(1)} %bitcast.22), channel_id=1, source_target_pairs={{0,2},{2,0},{1,3},{3,1},{4,6},{6,4},{5,7},{7,5},{8,10},{10,8},{9,1... | collective-permute-start | bytes 3145736 | tf_op jit(solution)/shard_map/ppermute | solution.py:21
  42.3 56.1 %collective-permute-start.3 = (bf16[1,8,4,32,128]{4,3,2,1,0:T(8,128)(2,1)S(1)}, bf16[1,8,4,32,128]{4,3,2,1,0:T(8,128)(2,1)S(1)}, u32[]{:S(2)}, u32[]{:S(2)}) collective-permute-start(bf16[1,8,4,32,128]{4,3,2,1,0:T(8,128)(2,1)S(1)} %bitcast.24), channel_id=1, source_target_pairs={{0,2},{2,0},{128,130},{130,128},{1,3},{3,1},{129,131},{131,129},{4... | collective-permute-start | bytes 786440 | tf_op jit(solution)/shard_map/ppermute | solution.py:21
  98.4 25.1 %collective-permute-start.11 = (bf16[2,8,4,32,128]{4,3,2,1,0:T(8,128)(2,1)S(1)}, bf16[2,8,4,32,128]{4,3,2,1,0:T(8,128)(2,1)S(1)}, u32[]{:S(2)}, u32[]{:S(2)}) collective-permute-start(bf16[2,8,4,32,128]{4,3,2,1,0:T(8,128)(2,1)S(1)} %pad_maximum_fusion.1.refs_0_), channel_id=1, source_target_pairs={{0,1},{1,0},{2,3},{3,2},{4,5},{5,4},{6,7},{7,6},{8,9},{9,8},{10,11... | collective-permute-start | bytes 1572872 | tf_op jit(solution)/shard_map/ppermute | solution.py:21
  98.5 24.8 %collective-permute-start.7 = (bf16[2,8,4,32,128]{4,3,2,1,0:T(8,128)(2,1)S(1)}, bf16[2,8,4,32,128]{4,3,2,1,0:T(8,128)(2,1)S(1)}, u32[]{:S(2)}, u32[]{:S(2)}) collective-permute-start(bf16[2,8,4,32,128]{4,3,2,1,0:T(8,128)(2,1)S(1)} %pad_maximum_fusion.1.refs_0_), channel_id=1, source_target_pairs={{0,96},{32,64},{64,32},{96,0},{1,97},{33,65},{65,33},{97,1},{2,98}... | collective-permute-start | bytes 1572872 | tf_op jit(solution)/shard_map/ppermute | solution.py:21
  101.6 23.5 %collective-permute-start.4 = (bf16[2,8,4,32,128]{4,3,2,1,0:T(8,128)(2,1)S(1)}, bf16[2,8,4,32,128]{4,3,2,1,0:T(8,128)(2,1)S(1)}, u32[]{:S(2)}, u32[]{:S(2)}) collective-permute-start(bf16[2,8,4,32,128]{4,3,2,1,0:T(8,128)(2,1)S(1)} %pad_maximum_fusion.1.refs_0_), channel_id=1, source_target_pairs={{0,130},{2,128},{128,2},{130,0},{1,131},{3,129},{129,3},{131,1},{4... | collective-permute-start | bytes 1572872 | tf_op jit(solution)/shard_map/ppermute | solution.py:21
  103.9 66.3 %collective-permute-start.20 = (bf16[2,8,128,512]{3,2,1,0:T(8,128)(2,1)S(1)}, bf16[2,8,128,512]{3,2,1,0:T(8,128)(2,1)}, u32[]{:S(2)}, u32[]{:S(2)}) collective-permute-start(bf16[2,8,128,512]{3,2,1,0:T(8,128)(2,1)S(1)} %pad_maximum_fusion.refs_16_), channel_id=1, source_target_pairs={{0,1},{1,0},{2,3},{3,2},{4,5},{5,4},{6,7},{7,6},{8,9},{9,8},{10,11... | collective-permute-start | bytes 6291464 | tf_op jit(solution)/shard_map/ppermute | solution.py:21
  104.0 23.2 %collective-permute-start.5 = (bf16[2,8,4,32,128]{4,3,2,1,0:T(8,128)(2,1)S(1)}, bf16[2,8,4,32,128]{4,3,2,1,0:T(8,128)(2,1)S(1)}, u32[]{:S(2)}, u32[]{:S(2)}) collective-permute-start(bf16[2,8,4,32,128]{4,3,2,1,0:T(8,128)(2,1)S(1)} %pad_maximum_fusion.1.refs_0_), channel_id=1, source_target_pairs={{0,32},{32,0},{64,96},{96,64},{1,33},{33,1},{65,97},{97,65},{2,34}... | collective-permute-start | bytes 1572872 | tf_op jit(solution)/shard_map/ppermute | solution.py:21
  123.3 4.7 %collective-permute-start.17 = (bf16[2,8,4,32,128]{4,3,2,1,0:T(8,128)(2,1)S(1)}, bf16[2,8,4,32,128]{4,3,2,1,0:T(8,128)(2,1)S(1)}, u32[]{:S(2)}, u32[]{:S(2)}) collective-permute-start(bf16[2,8,4,32,128]{4,3,2,1,0:T(8,128)(2,1)S(1)} %collective-permute-done.7.refs_6_), channel_id=1, source_target_pairs={{0,1},{1,0},{2,3},{3,2},{4,5},{5,4},{6,7},{7,6},{8,9},{9,8},{10,11... | collective-permute-start | bytes 1572872 | tf_op jit(solution)/shard_map/ppermute | solution.py:21
  123.5 17.9 %collective-permute-start.8 = (bf16[2,8,4,32,128]{4,3,2,1,0:T(8,128)(2,1)S(1)}, bf16[2,8,4,32,128]{4,3,2,1,0:T(8,128)(2,1)}, u32[]{:S(2)}, u32[]{:S(2)}) collective-permute-start(bf16[2,8,4,32,128]{4,3,2,1,0:T(8,128)(2,1)S(1)} %collective-permute-done.7.refs_6_), channel_id=1, source_target_pairs={{0,32},{32,0},{64,96},{96,64},{1,33},{33,1},{65,97},{97,65},{2,34}... | collective-permute-start | bytes 1572872 | tf_op jit(solution)/shard_map/ppermute | solution.py:21
  125.1 27.4 %collective-permute-start.6 = (bf16[2,8,4,32,128]{4,3,2,1,0:T(8,128)(2,1)S(1)}, bf16[2,8,4,32,128]{4,3,2,1,0:T(8,128)(2,1)}, u32[]{:S(2)}, u32[]{:S(2)}) collective-permute-start(bf16[2,8,4,32,128]{4,3,2,1,0:T(8,128)(2,1)S(1)} %collective-permute-done.4.refs_1_), channel_id=1, source_target_pairs={{0,32},{32,0},{64,96},{96,64},{1,33},{33,1},{65,97},{97,65},{2,34}... | collective-permute-start | bytes 1572872 | tf_op jit(solution)/shard_map/ppermute | solution.py:21
  127.2 25.4 %collective-permute-start.13 = (bf16[2,8,4,32,128]{4,3,2,1,0:T(8,128)(2,1)S(1)}, bf16[2,8,4,32,128]{4,3,2,1,0:T(8,128)(2,1)S(1)}, u32[]{:S(2)}, u32[]{:S(2)}) collective-permute-start(bf16[2,8,4,32,128]{4,3,2,1,0:T(8,128)(2,1)S(1)} %collective-permute-done.5.refs_2_), channel_id=1, source_target_pairs={{0,1},{1,0},{2,3},{3,2},{4,5},{5,4},{6,7},{7,6},{8,9},{9,8},{10,11... | collective-permute-start | bytes 1572872 | tf_op jit(solution)/shard_map/ppermute | solution.py:21
  128.8 24.5 %collective-permute-start.12 = (bf16[2,8,4,32,128]{4,3,2,1,0:T(8,128)(2,1)S(1)}, bf16[2,8,4,32,128]{4,3,2,1,0:T(8,128)(2,1)S(1)}, u32[]{:S(2)}, u32[]{:S(2)}) collective-permute-start(bf16[2,8,4,32,128]{4,3,2,1,0:T(8,128)(2,1)S(1)} %collective-permute-done.4.refs_1_), channel_id=1, source_target_pairs={{0,1},{1,0},{2,3},{3,2},{4,5},{5,4},{6,7},{7,6},{8,9},{9,8},{10,11... | collective-permute-start | bytes 1572872 | tf_op jit(solution)/shard_map/ppermute | solution.py:21
  141.3 15.1 %collective-permute-start.10 = (bf16[2,8,4,32,128]{4,3,2,1,0:T(8,128)(2,1)S(1)}, bf16[2,8,4,32,128]{4,3,2,1,0:T(8,128)(2,1)}, u32[]{:S(2)}, u32[]{:S(2)}) collective-permute-start(bf16[2,8,4,32,128]{4,3,2,1,0:T(8,128)(2,1)S(1)} %collective-permute-done.4.refs_1_), channel_id=1, source_target_pairs={{0,96},{32,64},{64,32},{96,0},{1,97},{33,65},{65,33},{97,1},{2,98}... | collective-permute-start | bytes 1572872 | tf_op jit(solution)/shard_map/ppermute | solution.py:21
  152.5 15.4 %collective-permute-start.9 = (bf16[2,8,4,32,128]{4,3,2,1,0:T(8,128)(2,1)}, bf16[2,8,4,32,128]{4,3,2,1,0:T(8,128)(2,1)}, u32[]{:S(2)}, u32[]{:S(2)}) collective-permute-start(bf16[2,8,4,32,128]{4,3,2,1,0:T(8,128)(2,1)} %collective-permute-done.6.refs_3_), channel_id=1, source_target_pairs={{0,96},{32,64},{64,32},{96,0},{1,97},{33,65},{65,33},{97,1},{2,98}... | collective-permute-start | bytes 1572872 | tf_op jit(solution)/shard_map/ppermute | solution.py:21
  153.4 14.6 %collective-permute-start.14 = (bf16[2,8,4,32,128]{4,3,2,1,0:T(8,128)(2,1)}, bf16[2,8,4,32,128]{4,3,2,1,0:T(8,128)(2,1)}, u32[]{:S(2)}, u32[]{:S(2)}) collective-permute-start(bf16[2,8,4,32,128]{4,3,2,1,0:T(8,128)(2,1)} %collective-permute-done.6.refs_3_), channel_id=1, source_target_pairs={{0,1},{1,0},{2,3},{3,2},{4,5},{5,4},{6,7},{7,6},{8,9},{9,8},{10,11... | collective-permute-start | bytes 1572872 | tf_op jit(solution)/shard_map/ppermute | solution.py:21
  154.2 13.8 %collective-permute-start.15 = (bf16[2,8,4,32,128]{4,3,2,1,0:T(8,128)(2,1)}, bf16[2,8,4,32,128]{4,3,2,1,0:T(8,128)(2,1)}, u32[]{:S(2)}, u32[]{:S(2)}) collective-permute-start(bf16[2,8,4,32,128]{4,3,2,1,0:T(8,128)(2,1)} %collective-permute-done.8.refs_4_), channel_id=1, source_target_pairs={{0,1},{1,0},{2,3},{3,2},{4,5},{5,4},{6,7},{7,6},{8,9},{9,8},{10,11... | collective-permute-start | bytes 1572872 | tf_op jit(solution)/shard_map/ppermute | solution.py:21
  156.4 11.5 %collective-permute-start.18 = (bf16[2,8,4,32,128]{4,3,2,1,0:T(8,128)(2,1)}, bf16[2,8,4,32,128]{4,3,2,1,0:T(8,128)(2,1)}, u32[]{:S(2)}, u32[]{:S(2)}) collective-permute-start(bf16[2,8,4,32,128]{4,3,2,1,0:T(8,128)(2,1)} %collective-permute-done.10.refs_7_), channel_id=1, source_target_pairs={{0,1},{1,0},{2,3},{3,2},{4,5},{5,4},{6,7},{7,6},{8,9},{9,8},{10,11... | collective-permute-start | bytes 1572872 | tf_op jit(solution)/shard_map/ppermute | solution.py:21
  167.9 2.3 collective-permute-start.16
  170.1 1.0 copy-start.1
  (11 other events, 10.0 us)
where the time goes:
time: 228 us; the launch traced here: 226 us
  waiting for transfers between devices  115 us (50%)
  blocking collectives  31.9 us (14%)
  starting transfers between devices  31.6 us (14%)
  Pallas kernels  31.4 us (14%)
  local copies, waits for them, and re-layouts  12 us (5%)
  matrix products  3.86 us (2%)
    ppermute x21, waiting for transfers between devices, swap(): return lax.ppermute(block, axis, [(i, i ^ flip) for i in range(count)])  115 us
    all_to_all x1, blocking collectives, body(): lax.all_to_all(part.reshape(lanes, npair // lanes, AROWS * nb), LANE, 0,...  31.9 us
    ppermute x21, starting transfers between devices, swap(): return lax.ppermute(block, axis, [(i, i ^ flip) for i in range(count)])  19.5 us
    pallas_call x1, Pallas kernels, make_ladder(): pl.pallas_call(ladder_kernel, in_specs=[pl.BlockSpec(memory_space=pltpu.S...  16.9 us
    pallas_call x2, Pallas kernels, make_vec(): pl.pallas_call(vec_kernel, grid=(2 * PHASES,), in_specs=ins, out_specs=pl...  14.5 us
    all_to_all x1, starting transfers between devices, body(): got = lax.all_to_all(send, EVERY, 0, 0, tiled=True)  12 us
    unnamed x26, local copies, waits for them, and re-layouts  11 us
  transfers between devices with their start and end apart: 22, of which 10 were waited for; matrix products, arithmetic and copies ran while one was open for 0% of the time, Pallas kernels for 6%

commit v1 on v0

--- a/solution.py
+++ b/solution.py
@@ -105,9 +105,8 @@
         return pltpu.make_async_copy(got_hbm.at[at], got_ref.at[sy, sx], got_sem.at[sy, sx])
 
     def side_copy(i, half):
-        source = 1 - half if i < count - nco and i % nyh else half
         return pltpu.make_async_copy(
-            side_hbm[i].at[source], sides[i].at[half], side_sem.at[i, half]
+            side_hbm[i].at[half], sides[i].at[half], side_sem.at[i, half]
         )
 
     order = [(sx, sy) for sx in range(nx) for sy in range(nyh)]
@@ -218,8 +217,9 @@
     got = got.reshape(2, 4, 8, 2, 2, dl, nl, nb)
     pair = pair[None]
     near = swap(pair, ("yh", "yl"), 1)
-    same = [jnp.concatenate([pair, near], axis=0), None]
-    same[1] = swap(same[0], ("yh", "yl"), 3)
+    far = swap(pair, ("yh", "yl"), 2)
+    cross = swap(pair, ("yh", "yl"), 3)
+    same = [jnp.concatenate([pair, near], axis=0), jnp.concatenate([far, cross], axis=0)]
     one = [swap(same[0], "x", 1), None]
     three = [swap(same[0], "x", 3), None]
     one[1] = swap(same[1], "x", 1)

time: 228 us -> 223 us (0.978)
  waiting for transfers between devices: 115 us -> 111 us
    ppermute x21 -> x22, waiting for transfers between devices: 115 us -> 111 us  [swap(): return lax.ppermute(block, axis, [(i, i ^ flip) for i in range(count)])]
    ppermute x21 -> x22, starting transfers between devices: 19.5 us -> 19.1 us  [swap(): return lax.ppermute(block, axis, [(i, i ^ flip) for i in range(count)])]
    unnamed x26 -> x27, local copies, waits for them, and re-layouts: 11 us -> 11.1 us
  transfers between devices with their start and end apart: 22 -> 23, of which waited for: 10 -> 10; matrix products, arithmetic and copies ran while one was open for 0% -> 0% of each run, Pallas kernels for 6% -> 7%
where the time goes in v1:
time: 223 us; the launch traced here: 221 us
  waiting for transfers between devices  111 us (50%)
  Pallas kernels  31.4 us (14%)
  blocking collectives  31.4 us (14%)
  starting transfers between devices  31.2 us (14%)
  local copies, waits for them, and re-layouts  12.1 us (5%)
  matrix products  3.86 us (2%)
    ppermute x22, waiting for transfers between devices, swap(): return lax.ppermute(block, axis, [(i, i ^ flip) for i in range(count)])  111 us
    all_to_all x1, blocking collectives, body(): lax.all_to_all(part.reshape(lanes, npair // lanes, AROWS * nb), LANE, 0,...  31.4 us
    ppermute x22, starting transfers between devices, swap(): return lax.ppermute(block, axis, [(i, i ^ flip) for i in range(count)])  19.1 us
    pallas_call x1, Pallas kernels, make_ladder(): pl.pallas_call(ladder_kernel, in_specs=[pl.BlockSpec(memory_space=pltpu.S...  16.9 us
    pallas_call x2, Pallas kernels, make_vec(): pl.pallas_call(vec_kernel, grid=(2 * PHASES,), in_specs=ins, out_specs=pl...  14.5 us
    all_to_all x1, starting transfers between devices, body(): got = lax.all_to_all(send, EVERY, 0, 0, tiled=True)  12 us
    unnamed x27, local copies, waits for them, and re-layouts  11.1 us
  transfers between devices with their start and end apart: 23, of which 10 were waited for; matrix products, arithmetic and copies ran while one was open for 0% of the time, Pallas kernels for 7%

profile of v1, /device:TPU:0, one launch (start us, length us, event | category | flops | bytes accessed | tf_op | source)
XLA Modules:
  0.0 221.1 jit_solution(8259523966841509171)
XLA Ops:
  0.0 3.9 %fusion = bf16[4,32,128]{2,0,1:T(4,128)(2,1)S(1)} fusion(bf16[32,768,128]{2,1,0:T(8,128)(2,1)} %half_ref.1, bf16[768,512]{1,0:T(8,128)(2,1)} %mo_ref.3), kind=kOutput, calls=%fused_computation.4 | convolution fusion | flops 25165824 | bytes 6520832 | tf_op jit(solution)/shard_map/lmc,ma->alc/dot_general | solution.py:203
  4.2 7.3 %vec.2.refs_0_ = bf16[64,4,2,32,128]{4,3,2,1,0:T(8,128)(2,1)} custom-call(bf16[32,768,128]{2,1,0:T(8,128)(2,1)} %half_ref.1, bf16[768,512]{1,0:T(8,128)(2,1)} %mo_ref.3), custom_call_target="tpu_custom_call" | custom-call | flops 1610612736 | bytes 5242880 | tf_op jit(solution)/shard_map/vec/pallas_call | solution.py:73
  11.5 3.4 %collective-permute-start.1 = (bf16[2,4,32,128]{3,2,1,0:T(8,128)(2,1)S(1)}, bf16[2,4,32,128]{3,2,1,0:T(8,128)(2,1)S(1)}, u32[]{:S(2)}, u32[]{:S(2)}) collective-permute-start(bf16[2,4,32,128]{3,2,1,0:T(8,128)(2,1)S(1)} %pad_maximum_fusion.4), channel_id=1, source_target_pairs={{0,8},{4,12},{8,0},{12,4},{16,24},{20,28},{24,16},{28,20},{1,9},{5... | collective-permute-start | bytes 196616 | tf_op jit(solution)/shard_map/ppermute | solution.py:21
  14.8 2.3 %collective-permute-done.1 = bf16[2,4,32,128]{3,2,1,0:T(8,128)(2,1)S(1)} collective-permute-done((bf16[2,4,32,128]{3,2,1,0:T(8,128)(2,1)S(1)}, bf16[2,4,32,128]{3,2,1,0:T(8,128)(2,1)S(1)}, u32[]{:S(2)}, u32[]{:S(2)}) %collective-permute-start.1) | collective-permute-done | bytes 65568 | tf_op jit(solution)/shard_map/ppermute | solution.py:21
  17.1 5.5 %collective-permute-start.2 = (bf16[4,4,32,128]{3,2,1,0:T(8,128)(2,1)S(1)}, bf16[4,4,32,128]{3,2,1,0:T(8,128)(2,1)S(1)}, u32[]{:S(2)}, u32[]{:S(2)}) collective-permute-start(bf16[4,4,32,128]{3,2,1,0:T(8,128)(2,1)S(1)} %pad_maximum_fusion.3), channel_id=1, source_target_pairs={{0,28},{4,24},{8,20},{12,16},{16,12},{20,8},{24,4},{28,0},{1,29},{... | collective-permute-start | bytes 393224 | tf_op jit(solution)/shard_map/ppermute | solution.py:21
  22.6 7.2 %vec.3 = bf16[64,4,2,32,128]{4,3,2,1,0:T(8,128)(2,1)} custom-call(bf16[32,768,128]{2,1,0:T(8,128)(2,1)} %half_ref.1, bf16[768,512]{1,0:T(8,128)(2,1)} %mo_ref.3, bf16[64,4,2,32,128]{4,3,2,1,0:T(8,128)(2,1)} %vec.2.refs_0_), custom_call_target="tpu_custom_call", output_to_operand_aliasing={{}: (2, {})} | custom-call | flops 1610612736 | bytes 5242880 | tf_op jit(solution)/shard_map/vec/pallas_call | solution.py:73
  29.9 12.0 %all-to-all-start = ((bf16[256,64,128]{2,1,0:T(8,128)(2,1)}), bf16[256,64,128]{2,1,0:T(8,128)(2,1)}, u32[]{:S(2)}, u32[]{:S(2)}) async-start(bf16[256,64,128]{2,1,0:T(8,128)(2,1)} %bitcast.21), calls=%async_computation | async-start | bytes 8388608 | tf_op jit(solution)/shard_map/all_to_all | solution.py:216
  42.3 2.0 collective-permute-start.3
  44.3 54.0 %collective-permute-done.3 = bf16[1,8,4,32,128]{4,3,2,1,0:T(8,128)(2,1)S(1)} collective-permute-done((bf16[1,8,4,32,128]{4,3,2,1,0:T(8,128)(2,1)S(1)}, bf16[1,8,4,32,128]{4,3,2,1,0:T(8,128)(2,1)S(1)}, u32[]{:S(2)}, u32[]{:S(2)}) %collective-permute-start.3) | collective-permute-done | bytes 262176 | tf_op jit(solution)/shard_map/ppermute | solution.py:21
  98.5 3.1 %collective-permute-start.8 = (bf16[2,8,4,32,128]{4,3,2,1,0:T(8,128)(2,1)S(1)}, bf16[2,8,4,32,128]{4,3,2,1,0:T(8,128)(2,1)S(1)}, u32[]{:S(2)}, u32[]{:S(2)}) collective-permute-start(bf16[2,8,4,32,128]{4,3,2,1,0:T(8,128)(2,1)S(1)} %pad_maximum_fusion.1.refs_0_), channel_id=1, source_target_pairs={{0,96},{32,64},{64,32},{96,0},{1,97},{33,65},{65,33},{97,1},{2,98}... | collective-permute-start | bytes 1572872 | tf_op jit(solution)/shard_map/ppermute | solution.py:21
  101.9 2.8 %collective-permute-start.4 = (bf16[1,8,4,32,128]{4,3,2,1,0:T(8,128)(2,1)S(1)}, bf16[1,8,4,32,128]{4,3,2,1,0:T(8,128)(2,1)S(1)}, u32[]{:S(2)}, u32[]{:S(2)}) collective-permute-start(bf16[1,8,4,32,128]{4,3,2,1,0:T(8,128)(2,1)S(1)} %bitcast.26), channel_id=1, source_target_pairs={{0,128},{2,130},{128,0},{130,2},{1,129},{3,131},{129,1},{131,3},{4... | collective-permute-start | bytes 786440 | tf_op jit(solution)/shard_map/ppermute | solution.py:21
  105.7 11.6 %collective-permute-done.4 = bf16[1,8,4,32,128]{4,3,2,1,0:T(8,128)(2,1)S(1)} collective-permute-done((bf16[1,8,4,32,128]{4,3,2,1,0:T(8,128)(2,1)S(1)}, bf16[1,8,4,32,128]{4,3,2,1,0:T(8,128)(2,1)S(1)}, u32[]{:S(2)}, u32[]{:S(2)}) %collective-permute-start.4) | collective-permute-done | bytes 262176 | tf_op jit(solution)/shard_map/ppermute | solution.py:21
  117.3 10.0 %collective-permute-done.5 = bf16[1,8,4,32,128]{4,3,2,1,0:T(8,128)(2,1)S(1)} collective-permute-done((bf16[1,8,4,32,128]{4,3,2,1,0:T(8,128)(2,1)S(1)}, bf16[1,8,4,32,128]{4,3,2,1,0:T(8,128)(2,1)S(1)}, u32[]{:S(2)}, u32[]{:S(2)}) %collective-permute-start.5) | collective-permute-done | bytes 262176 | tf_op jit(solution)/shard_map/ppermute | solution.py:21
  128.5 9.9 %collective-permute-done.6.refs_2_ = bf16[2,8,4,32,128]{4,3,2,1,0:T(8,128)(2,1)S(1)} collective-permute-done((bf16[2,8,4,32,128]{4,3,2,1,0:T(8,128)(2,1)S(1)}, bf16[2,8,4,32,128]{4,3,2,1,0:T(8,128)(2,1)S(1)}, u32[]{:S(2)}, u32[]{:S(2)}) %collective-permute-start.6) | collective-permute-done | bytes 524320 | tf_op jit(solution)/shard_map/ppermute | solution.py:21
  139.9 4.0 %collective-permute-done.11.refs_7_ = bf16[2,8,4,32,128]{4,3,2,1,0:T(8,128)(2,1)} collective-permute-done((bf16[2,8,4,32,128]{4,3,2,1,0:T(8,128)(2,1)S(1)}, bf16[2,8,4,32,128]{4,3,2,1,0:T(8,128)(2,1)}, u32[]{:S(2)}, u32[]{:S(2)}) %collective-permute-start.11) | collective-permute-done | bytes 524320 | tf_op jit(solution)/shard_map/ppermute | solution.py:21
  144.7 5.0 %collective-permute-done.7.refs_3_ = bf16[2,8,4,32,128]{4,3,2,1,0:T(8,128)(2,1)} collective-permute-done((bf16[2,8,4,32,128]{4,3,2,1,0:T(8,128)(2,1)S(1)}, bf16[2,8,4,32,128]{4,3,2,1,0:T(8,128)(2,1)}, u32[]{:S(2)}, u32[]{:S(2)}) %collective-permute-start.7) | collective-permute-done | bytes 524320 | tf_op jit(solution)/shard_map/ppermute | solution.py:21
  150.5 9.6 %collective-permute-done.9.refs_4_ = bf16[2,8,4,32,128]{4,3,2,1,0:T(8,128)(2,1)} collective-permute-done((bf16[2,8,4,32,128]{4,3,2,1,0:T(8,128)(2,1)S(1)}, bf16[2,8,4,32,128]{4,3,2,1,0:T(8,128)(2,1)}, u32[]{:S(2)}, u32[]{:S(2)}) %collective-permute-start.9) | collective-permute-done | bytes 524320 | tf_op jit(solution)/shard_map/ppermute | solution.py:21
  161.4 2.1 collective-permute-done.10.refs_5_
  163.6 2.2 collective-permute-done.17.refs_13_
  167.9 1.0 copy-done.5
  168.9 1.0 copy-done.7
  171.0 1.0 copy-done.11
  172.0 16.9 %ladder.1 = bf16[512,512]{1,0:T(8,128)(2,1)S(1)} custom-call(s32[3]{0:T(128)S(1)} %pad_add_fusion.where_ref, bf16[2,4,8,2,2,2,32,128]{7,6,5,4,3,2,1,0:T(8,128)(2,1)} %bitcast.6.got_hbm, bf16[2,8,4,32,128]{4,3,2,1,0:T(8,128)(2,1)S(1)} %pad_maximum_fusion.1.refs_0_, bf16[2,8,4,32,128]{4,3,2,1,0:T(8,128)(2,1)S(1)} %constant_dynamic-update-slice_fusion.refs_1_, ...), custom_call_target="tpu_custom_call" | custom-call | tf_op jit(solution)/shard_map/ladder/pallas_call | solution.py:176
  189.0 31.4 %all_to_all.10 = bf16[64,8,512]{2,1,0:T(8,128)(2,1)S(1)} all-to-all(bf16[64,8,512]{2,1,0:T(8,128)(2,1)S(1)} %bitcast.20), channel_id=1, replica_groups=mesh['yh'=2,'x'=4,'z'=8,'yl'=2,'co'=2] {'yh','x','z'}, dimensions={0} | all-to-all | bytes 1048576 | tf_op jit(solution)/shard_map/all_to_all | solution.py:235
  (65 shorter events, 11.9 us)
Async XLA Ops:
  3.9 7.6 %collective-permute-start = (bf16[1,4,32,128]{3,2,1,0:T(8,128)(2,1)S(1)}, bf16[1,4,32,128]{3,2,1,0:T(8,128)(2,1)S(1)}, u32[]{:S(2)}, u32[]{:S(2)}) collective-permute-start(bf16[1,4,32,128]{3,2,1,0:T(8,128)(2,1)S(1)} %bitcast.28), channel_id=1, source_target_pairs={{0,4},{4,0},{8,12},{12,8},{16,20},{20,16},{24,28},{28,24},{1,5},{5... | collective-permute-start | bytes 98312 | tf_op jit(solution)/shard_map/ppermute | solution.py:21
  11.5 5.6 %collective-permute-start.1 = (bf16[2,4,32,128]{3,2,1,0:T(8,128)(2,1)S(1)}, bf16[2,4,32,128]{3,2,1,0:T(8,128)(2,1)S(1)}, u32[]{:S(2)}, u32[]{:S(2)}) collective-permute-start(bf16[2,4,32,128]{3,2,1,0:T(8,128)(2,1)S(1)} %pad_maximum_fusion.4), channel_id=1, source_target_pairs={{0,8},{4,12},{8,0},{12,4},{16,24},{20,28},{24,16},{28,20},{1,9},{5... | collective-permute-start | bytes 196616 | tf_op jit(solution)/shard_map/ppermute | solution.py:21
  17.1 12.7 %collective-permute-start.2 = (bf16[4,4,32,128]{3,2,1,0:T(8,128)(2,1)S(1)}, bf16[4,4,32,128]{3,2,1,0:T(8,128)(2,1)S(1)}, u32[]{:S(2)}, u32[]{:S(2)}) collective-permute-start(bf16[4,4,32,128]{3,2,1,0:T(8,128)(2,1)S(1)} %pad_maximum_fusion.3), channel_id=1, source_target_pairs={{0,28},{4,24},{8,20},{12,16},{16,12},{20,8},{24,4},{28,0},{1,29},{... | collective-permute-start | bytes 393224 | tf_op jit(solution)/shard_map/ppermute | solution.py:21
  29.8 12.0 %copy-start.12 = (bf16[128,4,2,512]{3,2,1,0:T(2,128)(2,1)S(1)}, bf16[128,4,2,512]{3,2,1,0:T(2,128)(2,1)}, u32[]{:S(2)}) copy-start(bf16[128,4,2,512]{3,2,1,0:T(2,128)(2,1)} %param.5) | copy-start | bytes 3145732
  29.9 135.9 %all-to-all-start = ((bf16[256,64,128]{2,1,0:T(8,128)(2,1)}), bf16[256,64,128]{2,1,0:T(8,128)(2,1)}, u32[]{:S(2)}, u32[]{:S(2)}) async-start(bf16[256,64,128]{2,1,0:T(8,128)(2,1)} %bitcast.21), calls=%async_computation | async-start | bytes 8388608 | tf_op jit(solution)/shard_map/all_to_all | solution.py:216
  42.2 59.4 %collective-permute-start.20 = (bf16[1,8,128,512]{3,2,1,0:T(8,128)(2,1)S(1)}, bf16[1,8,128,512]{3,2,1,0:T(8,128)(2,1)S(1)}, u32[]{:S(2)}, u32[]{:S(2)}) collective-permute-start(bf16[1,8,128,512]{3,2,1,0:T(8,128)(2,1)S(1)} %bitcast.22), channel_id=1, source_target_pairs={{0,2},{2,0},{1,3},{3,1},{4,6},{6,4},{5,7},{7,5},{8,10},{10,8},{9,1... | collective-permute-start | bytes 3145736 | tf_op jit(solution)/shard_map/ppermute | solution.py:21
  42.3 56.1 %collective-permute-start.3 = (bf16[1,8,4,32,128]{4,3,2,1,0:T(8,128)(2,1)S(1)}, bf16[1,8,4,32,128]{4,3,2,1,0:T(8,128)(2,1)S(1)}, u32[]{:S(2)}, u32[]{:S(2)}) collective-permute-start(bf16[1,8,4,32,128]{4,3,2,1,0:T(8,128)(2,1)S(1)} %bitcast.24), channel_id=1, source_target_pairs={{0,2},{2,0},{128,130},{130,128},{1,3},{3,1},{129,131},{131,129},{4... | collective-permute-start | bytes 786440 | tf_op jit(solution)/shard_map/ppermute | solution.py:21
  98.4 29.2 %collective-permute-start.12 = (bf16[2,8,4,32,128]{4,3,2,1,0:T(8,128)(2,1)S(1)}, bf16[2,8,4,32,128]{4,3,2,1,0:T(8,128)(2,1)S(1)}, u32[]{:S(2)}, u32[]{:S(2)}) collective-permute-start(bf16[2,8,4,32,128]{4,3,2,1,0:T(8,128)(2,1)S(1)} %pad_maximum_fusion.1.refs_0_), channel_id=1, source_target_pairs={{0,1},{1,0},{2,3},{3,2},{4,5},{5,4},{6,7},{7,6},{8,9},{9,8},{10,11... | collective-permute-start | bytes 1572872 | tf_op jit(solution)/shard_map/ppermute | solution.py:21
  98.5 29.9 %collective-permute-start.8 = (bf16[2,8,4,32,128]{4,3,2,1,0:T(8,128)(2,1)S(1)}, bf16[2,8,4,32,128]{4,3,2,1,0:T(8,128)(2,1)S(1)}, u32[]{:S(2)}, u32[]{:S(2)}) collective-permute-start(bf16[2,8,4,32,128]{4,3,2,1,0:T(8,128)(2,1)S(1)} %pad_maximum_fusion.1.refs_0_), channel_id=1, source_target_pairs={{0,96},{32,64},{64,32},{96,0},{1,97},{33,65},{65,33},{97,1},{2,98}... | collective-permute-start | bytes 1572872 | tf_op jit(solution)/shard_map/ppermute | solution.py:21
  101.8 64.0 %collective-permute-start.21 = (bf16[2,8,128,512]{3,2,1,0:T(8,128)(2,1)S(1)}, bf16[2,8,128,512]{3,2,1,0:T(8,128)(2,1)}, u32[]{:S(2)}, u32[]{:S(2)}) collective-permute-start(bf16[2,8,128,512]{3,2,1,0:T(8,128)(2,1)S(1)} %pad_maximum_fusion.refs_16_), channel_id=1, source_target_pairs={{0,1},{1,0},{2,3},{3,2},{4,5},{5,4},{6,7},{7,6},{8,9},{9,8},{10,11... | collective-permute-start | bytes 6291464 | tf_op jit(solution)/shard_map/ppermute | solution.py:21
  101.9 15.4 %collective-permute-start.4 = (bf16[1,8,4,32,128]{4,3,2,1,0:T(8,128)(2,1)S(1)}, bf16[1,8,4,32,128]{4,3,2,1,0:T(8,128)(2,1)S(1)}, u32[]{:S(2)}, u32[]{:S(2)}) collective-permute-start(bf16[1,8,4,32,128]{4,3,2,1,0:T(8,128)(2,1)S(1)} %bitcast.26), channel_id=1, source_target_pairs={{0,128},{2,130},{128,0},{130,2},{1,129},{3,131},{129,1},{131,3},{4... | collective-permute-start | bytes 786440 | tf_op jit(solution)/shard_map/ppermute | solution.py:21
  104.7 22.6 %collective-permute-start.5 = (bf16[1,8,4,32,128]{4,3,2,1,0:T(8,128)(2,1)S(1)}, bf16[1,8,4,32,128]{4,3,2,1,0:T(8,128)(2,1)S(1)}, u32[]{:S(2)}, u32[]{:S(2)}) collective-permute-start(bf16[1,8,4,32,128]{4,3,2,1,0:T(8,128)(2,1)S(1)} %bitcast.27), channel_id=1, source_target_pairs={{0,130},{2,128},{128,2},{130,0},{1,131},{3,129},{129,3},{131,1},{4... | collective-permute-start | bytes 786440 | tf_op jit(solution)/shard_map/ppermute | solution.py:21
  117.3 21.1 %collective-permute-start.6 = (bf16[2,8,4,32,128]{4,3,2,1,0:T(8,128)(2,1)S(1)}, bf16[2,8,4,32,128]{4,3,2,1,0:T(8,128)(2,1)S(1)}, u32[]{:S(2)}, u32[]{:S(2)}) collective-permute-start(bf16[2,8,4,32,128]{4,3,2,1,0:T(8,128)(2,1)S(1)} %pad_maximum_fusion.1.refs_0_), channel_id=1, source_target_pairs={{0,32},{32,0},{64,96},{96,64},{1,33},{33,1},{65,97},{97,65},{2,34}... | collective-permute-start | bytes 1572872 | tf_op jit(solution)/shard_map/ppermute | solution.py:21
  127.3 11.0 %collective-permute-start.13 = (bf16[2,8,4,32,128]{4,3,2,1,0:T(8,128)(2,1)S(1)}, bf16[2,8,4,32,128]{4,3,2,1,0:T(8,128)(2,1)S(1)}, u32[]{:S(2)}, u32[]{:S(2)}) collective-permute-start(bf16[2,8,4,32,128]{4,3,2,1,0:T(8,128)(2,1)S(1)} %constant_dynamic-update-slice_fusion.refs_1_), channel_id=1, source_target_pairs={{0,1},{1,0},{2,3},{3,2},{4,5},{5,4},{6,7},{7,6},{8,9},{9,8},{10,11... | collective-permute-start | bytes 1572872 | tf_op jit(solution)/shard_map/ppermute | solution.py:21
  128.5 15.4 %collective-permute-start.11 = (bf16[2,8,4,32,128]{4,3,2,1,0:T(8,128)(2,1)S(1)}, bf16[2,8,4,32,128]{4,3,2,1,0:T(8,128)(2,1)}, u32[]{:S(2)}, u32[]{:S(2)}) collective-permute-start(bf16[2,8,4,32,128]{4,3,2,1,0:T(8,128)(2,1)S(1)} %constant_dynamic-update-slice_fusion.refs_1_), channel_id=1, source_target_pairs={{0,96},{32,64},{64,32},{96,0},{1,97},{33,65},{65,33},{97,1},{2,98}... | collective-permute-start | bytes 1572872 | tf_op jit(solution)/shard_map/ppermute | solution.py:21
  128.5 21.2 %collective-permute-start.7 = (bf16[2,8,4,32,128]{4,3,2,1,0:T(8,128)(2,1)S(1)}, bf16[2,8,4,32,128]{4,3,2,1,0:T(8,128)(2,1)}, u32[]{:S(2)}, u32[]{:S(2)}) collective-permute-start(bf16[2,8,4,32,128]{4,3,2,1,0:T(8,128)(2,1)S(1)} %constant_dynamic-update-slice_fusion.refs_1_), channel_id=1, source_target_pairs={{0,32},{32,0},{64,96},{96,64},{1,33},{33,1},{65,97},{97,65},{2,34}... | collective-permute-start | bytes 1572872 | tf_op jit(solution)/shard_map/ppermute | solution.py:21
  138.3 11.3 %collective-permute-start.18 = (bf16[2,8,4,32,128]{4,3,2,1,0:T(8,128)(2,1)S(1)}, bf16[2,8,4,32,128]{4,3,2,1,0:T(8,128)(2,1)S(1)}, u32[]{:S(2)}, u32[]{:S(2)}) collective-permute-start(bf16[2,8,4,32,128]{4,3,2,1,0:T(8,128)(2,1)S(1)} %collective-permute-done.8.refs_6_), channel_id=1, source_target_pairs={{0,1},{1,0},{2,3},{3,2},{4,5},{5,4},{6,7},{7,6},{8,9},{9,8},{10,11... | collective-permute-start | bytes 1572872 | tf_op jit(solution)/shard_map/ppermute | solution.py:21
  139.1 21.0 %collective-permute-start.9 = (bf16[2,8,4,32,128]{4,3,2,1,0:T(8,128)(2,1)S(1)}, bf16[2,8,4,32,128]{4,3,2,1,0:T(8,128)(2,1)}, u32[]{:S(2)}, u32[]{:S(2)}) collective-permute-start(bf16[2,8,4,32,128]{4,3,2,1,0:T(8,128)(2,1)S(1)} %collective-permute-done.8.refs_6_), channel_id=1, source_target_pairs={{0,32},{32,0},{64,96},{96,64},{1,33},{33,1},{65,97},{97,65},{2,34}... | collective-permute-start | bytes 1572872 | tf_op jit(solution)/shard_map/ppermute | solution.py:21
  143.9 16.2 %collective-permute-start.14 = (bf16[2,8,4,32,128]{4,3,2,1,0:T(8,128)(2,1)S(1)}, bf16[2,8,4,32,128]{4,3,2,1,0:T(8,128)(2,1)S(1)}, u32[]{:S(2)}, u32[]{:S(2)}) collective-permute-start(bf16[2,8,4,32,128]{4,3,2,1,0:T(8,128)(2,1)S(1)} %collective-permute-done.6.refs_2_), channel_id=1, source_target_pairs={{0,1},{1,0},{2,3},{3,2},{4,5},{5,4},{6,7},{7,6},{8,9},{9,8},{10,11... | collective-permute-start | bytes 1572872 | tf_op jit(solution)/shard_map/ppermute | solution.py:21
  149.7 13.9 %collective-permute-start.10 = (bf16[2,8,4,32,128]{4,3,2,1,0:T(8,128)(2,1)}, bf16[2,8,4,32,128]{4,3,2,1,0:T(8,128)(2,1)}, u32[]{:S(2)}, u32[]{:S(2)}) collective-permute-start(bf16[2,8,4,32,128]{4,3,2,1,0:T(8,128)(2,1)} %collective-permute-done.7.refs_3_), channel_id=1, source_target_pairs={{0,96},{32,64},{64,32},{96,0},{1,97},{33,65},{65,33},{97,1},{2,98}... | collective-permute-start | bytes 1572872 | tf_op jit(solution)/shard_map/ppermute | solution.py:21
  150.5 13.1 %collective-permute-start.15 = (bf16[2,8,4,32,128]{4,3,2,1,0:T(8,128)(2,1)}, bf16[2,8,4,32,128]{4,3,2,1,0:T(8,128)(2,1)}, u32[]{:S(2)}, u32[]{:S(2)}) collective-permute-start(bf16[2,8,4,32,128]{4,3,2,1,0:T(8,128)(2,1)} %collective-permute-done.7.refs_3_), channel_id=1, source_target_pairs={{0,1},{1,0},{2,3},{3,2},{4,5},{5,4},{6,7},{7,6},{8,9},{9,8},{10,11... | collective-permute-start | bytes 1572872 | tf_op jit(solution)/shard_map/ppermute | solution.py:21
  160.1 3.5 %collective-permute-start.19 = (bf16[2,8,4,32,128]{4,3,2,1,0:T(8,128)(2,1)}, bf16[2,8,4,32,128]{4,3,2,1,0:T(8,128)(2,1)}, u32[]{:S(2)}, u32[]{:S(2)}) collective-permute-start(bf16[2,8,4,32,128]{4,3,2,1,0:T(8,128)(2,1)} %collective-permute-done.11.refs_7_), channel_id=1, source_target_pairs={{0,1},{1,0},{2,3},{3,2},{4,5},{5,4},{6,7},{7,6},{8,9},{9,8},{10,11... | collective-permute-start | bytes 1572872 | tf_op jit(solution)/shard_map/ppermute | solution.py:21
  160.9 2.7 %collective-permute-start.16 = (bf16[2,8,4,32,128]{4,3,2,1,0:T(8,128)(2,1)}, bf16[2,8,4,32,128]{4,3,2,1,0:T(8,128)(2,1)}, u32[]{:S(2)}, u32[]{:S(2)}) collective-permute-start(bf16[2,8,4,32,128]{4,3,2,1,0:T(8,128)(2,1)} %collective-permute-done.9.refs_4_), channel_id=1, source_target_pairs={{0,1},{1,0},{2,3},{3,2},{4,5},{5,4},{6,7},{7,6},{8,9},{9,8},{10,11... | collective-permute-start | bytes 1572872 | tf_op jit(solution)/shard_map/ppermute | solution.py:21
  163.5 2.3 %collective-permute-start.17 = (bf16[2,8,4,32,128]{4,3,2,1,0:T(8,128)(2,1)}, bf16[2,8,4,32,128]{4,3,2,1,0:T(8,128)(2,1)}, u32[]{:S(2)}, u32[]{:S(2)}) collective-permute-start(bf16[2,8,4,32,128]{4,3,2,1,0:T(8,128)(2,1)} %collective-permute-done.10.refs_5_), channel_id=1, source_target_pairs={{0,1},{1,0},{2,3},{3,2},{4,5},{5,4},{6,7},{7,6},{8,9},{9,8},{10,11... | collective-permute-start | bytes 1572872 | tf_op jit(solution)/shard_map/ppermute | solution.py:21
  (12 other events, 11.1 us)

commit v2 on v1

--- a/solution.py
+++ b/solution.py
@@ -11,8 +11,8 @@
 GROUP = ("yl", "co")
 EVERY = LANE + GROUP
 PHASES = 2
-Z_STEPS = (1, 2, 7)
-Z_OFF = (0, 1, 2, 3, 7, 6, 5, 4)
+Z_STEPS = (1, 2, 6)
+Z_OFF = (0, 1, 2, 3, 6, 7, 4, 5)
 SIZES = {"yh": 2, "x": 4, "z": 8, "yl": 2, "co": 2}
 
 
@@ -46,7 +46,7 @@
     def _():
         first = (now - PHASES) * lanes * dl
 
-        @pl.loop(0, lanes, unroll=8)
+        @pl.loop(0, lanes, unroll=16)
         def _(lane):
             for j in range(dl):
                 for g in range(groups):

time: 223 us -> 223 us (level)
  transfers between devices with their start and end apart: 23 -> 23, of which waited for: 10 -> 10; matrix products, arithmetic and copies ran while one was open for 0% -> 0% of each run, Pallas kernels for 7% -> 6%
where the time goes in v2:
time: 223 us; the launch traced here: 221 us
  waiting for transfers between devices  110 us (49%)
  starting transfers between devices  31.4 us (14%)
  blocking collectives  31.4 us (14%)
  Pallas kernels  31.3 us (14%)
  local copies, waits for them, and re-layouts  12.1 us (5%)
  matrix products  3.86 us (2%)
    ppermute x22, waiting for transfers between devices, swap(): return lax.ppermute(block, axis, [(i, i ^ flip) for i in range(count)])  110 us
    all_to_all x1, blocking collectives, body(): lax.all_to_all(part.reshape(lanes, npair // lanes, AROWS * nb), LANE, 0,...  31.4 us
    ppermute x22, starting transfers between devices, swap(): return lax.ppermute(block, axis, [(i, i ^ flip) for i in range(count)])  19.1 us
    pallas_call x1, Pallas kernels, make_ladder(): pl.pallas_call(ladder_kernel, in_specs=[pl.BlockSpec(memory_space=pltpu.S...  16.9 us
    pallas_call x2, Pallas kernels, make_vec(): pl.pallas_call(vec_kernel, grid=(2 * PHASES,), in_specs=ins, out_specs=pl...  14.4 us
    all_to_all x1, starting transfers between devices, body(): got = lax.all_to_all(send, EVERY, 0, 0, tiled=True)  12.3 us
    unnamed x27, local copies, waits for them, and re-layouts  11.1 us
  transfers between devices with their start and end apart: 23, of which 10 were waited for; matrix products, arithmetic and copies ran while one was open for 0% of the time, Pallas kernels for 6%

profile of v2, /device:TPU:0, one launch (start us, length us, event | category | flops | bytes accessed | tf_op | source)
XLA Modules:
  0.0 221.0 jit_solution(7615343018144529546)
XLA Ops:
  0.0 3.9 %fusion = bf16[4,32,128]{2,0,1:T(4,128)(2,1)S(1)} fusion(bf16[32,768,128]{2,1,0:T(8,128)(2,1)} %half_ref.1, bf16[768,512]{1,0:T(8,128)(2,1)} %mo_ref.3), kind=kOutput, calls=%fused_computation.4 | convolution fusion | flops 25165824 | bytes 6520832 | tf_op jit(solution)/shard_map/lmc,ma->alc/dot_general | solution.py:203
  4.2 7.2 %vec.2.refs_0_ = bf16[64,4,2,32,128]{4,3,2,1,0:T(8,128)(2,1)} custom-call(bf16[32,768,128]{2,1,0:T(8,128)(2,1)} %half_ref.1, bf16[768,512]{1,0:T(8,128)(2,1)} %mo_ref.3), custom_call_target="tpu_custom_call" | custom-call | flops 1610612736 | bytes 5242880 | tf_op jit(solution)/shard_map/vec/pallas_call | solution.py:73
  11.4 3.4 %collective-permute-start.1 = (bf16[2,4,32,128]{3,2,1,0:T(8,128)(2,1)S(1)}, bf16[2,4,32,128]{3,2,1,0:T(8,128)(2,1)S(1)}, u32[]{:S(2)}, u32[]{:S(2)}) collective-permute-start(bf16[2,4,32,128]{3,2,1,0:T(8,128)(2,1)S(1)} %pad_maximum_fusion.4), channel_id=1, source_target_pairs={{0,8},{4,12},{8,0},{12,4},{16,24},{20,28},{24,16},{28,20},{1,9},{5... | collective-permute-start | bytes 196616 | tf_op jit(solution)/shard_map/ppermute | solution.py:21
  14.7 2.3 %collective-permute-done.1 = bf16[2,4,32,128]{3,2,1,0:T(8,128)(2,1)S(1)} collective-permute-done((bf16[2,4,32,128]{3,2,1,0:T(8,128)(2,1)S(1)}, bf16[2,4,32,128]{3,2,1,0:T(8,128)(2,1)S(1)}, u32[]{:S(2)}, u32[]{:S(2)}) %collective-permute-start.1) | collective-permute-done | bytes 65568 | tf_op jit(solution)/shard_map/ppermute | solution.py:21
  17.0 5.2 %collective-permute-start.2 = (bf16[4,4,32,128]{3,2,1,0:T(8,128)(2,1)S(1)}, bf16[4,4,32,128]{3,2,1,0:T(8,128)(2,1)S(1)}, u32[]{:S(2)}, u32[]{:S(2)}) collective-permute-start(bf16[4,4,32,128]{3,2,1,0:T(8,128)(2,1)S(1)} %pad_maximum_fusion.3), channel_id=1, source_target_pairs={{0,24},{4,28},{8,16},{12,20},{16,8},{20,12},{24,0},{28,4},{1,25},{... | collective-permute-start | bytes 393224 | tf_op jit(solution)/shard_map/ppermute | solution.py:21
  22.2 7.2 %vec.3 = bf16[64,4,2,32,128]{4,3,2,1,0:T(8,128)(2,1)} custom-call(bf16[32,768,128]{2,1,0:T(8,128)(2,1)} %half_ref.1, bf16[768,512]{1,0:T(8,128)(2,1)} %mo_ref.3, bf16[64,4,2,32,128]{4,3,2,1,0:T(8,128)(2,1)} %vec.2.refs_0_), custom_call_target="tpu_custom_call", output_to_operand_aliasing={{}: (2, {})} | custom-call | flops 1610612736 | bytes 5242880 | tf_op jit(solution)/shard_map/vec/pallas_call | solution.py:73
  29.5 12.3 %all-to-all-start = ((bf16[256,64,128]{2,1,0:T(8,128)(2,1)}), bf16[256,64,128]{2,1,0:T(8,128)(2,1)}, u32[]{:S(2)}, u32[]{:S(2)}) async-start(bf16[256,64,128]{2,1,0:T(8,128)(2,1)} %bitcast.21), calls=%async_computation | async-start | bytes 8388608 | tf_op jit(solution)/shard_map/all_to_all | solution.py:216
  42.2 2.0 collective-permute-start.3
  44.2 54.0 %collective-permute-done.3 = bf16[1,8,4,32,128]{4,3,2,1,0:T(8,128)(2,1)S(1)} collective-permute-done((bf16[1,8,4,32,128]{4,3,2,1,0:T(8,128)(2,1)S(1)}, bf16[1,8,4,32,128]{4,3,2,1,0:T(8,128)(2,1)S(1)}, u32[]{:S(2)}, u32[]{:S(2)}) %collective-permute-start.3) | collective-permute-done | bytes 262176 | tf_op jit(solution)/shard_map/ppermute | solution.py:21
  98.4 3.1 %collective-permute-start.8 = (bf16[2,8,4,32,128]{4,3,2,1,0:T(8,128)(2,1)S(1)}, bf16[2,8,4,32,128]{4,3,2,1,0:T(8,128)(2,1)S(1)}, u32[]{:S(2)}, u32[]{:S(2)}) collective-permute-start(bf16[2,8,4,32,128]{4,3,2,1,0:T(8,128)(2,1)S(1)} %pad_maximum_fusion.1.refs_0_), channel_id=1, source_target_pairs={{0,96},{32,64},{64,32},{96,0},{1,97},{33,65},{65,33},{97,1},{2,98}... | collective-permute-start | bytes 1572872 | tf_op jit(solution)/shard_map/ppermute | solution.py:21
  101.8 2.8 %collective-permute-start.4 = (bf16[1,8,4,32,128]{4,3,2,1,0:T(8,128)(2,1)S(1)}, bf16[1,8,4,32,128]{4,3,2,1,0:T(8,128)(2,1)S(1)}, u32[]{:S(2)}, u32[]{:S(2)}) collective-permute-start(bf16[1,8,4,32,128]{4,3,2,1,0:T(8,128)(2,1)S(1)} %bitcast.26), channel_id=1, source_target_pairs={{0,128},{2,130},{128,0},{130,2},{1,129},{3,131},{129,1},{131,3},{4... | collective-permute-start | bytes 786440 | tf_op jit(solution)/shard_map/ppermute | solution.py:21
  105.6 11.6 %collective-permute-done.4 = bf16[1,8,4,32,128]{4,3,2,1,0:T(8,128)(2,1)S(1)} collective-permute-done((bf16[1,8,4,32,128]{4,3,2,1,0:T(8,128)(2,1)S(1)}, bf16[1,8,4,32,128]{4,3,2,1,0:T(8,128)(2,1)S(1)}, u32[]{:S(2)}, u32[]{:S(2)}) %collective-permute-start.4) | collective-permute-done | bytes 262176 | tf_op jit(solution)/shard_map/ppermute | solution.py:21
  117.2 10.0 %collective-permute-done.5 = bf16[1,8,4,32,128]{4,3,2,1,0:T(8,128)(2,1)S(1)} collective-permute-done((bf16[1,8,4,32,128]{4,3,2,1,0:T(8,128)(2,1)S(1)}, bf16[1,8,4,32,128]{4,3,2,1,0:T(8,128)(2,1)S(1)}, u32[]{:S(2)}, u32[]{:S(2)}) %collective-permute-start.5) | collective-permute-done | bytes 262176 | tf_op jit(solution)/shard_map/ppermute | solution.py:21
  128.6 9.7 %collective-permute-done.6.refs_2_ = bf16[2,8,4,32,128]{4,3,2,1,0:T(8,128)(2,1)S(1)} collective-permute-done((bf16[2,8,4,32,128]{4,3,2,1,0:T(8,128)(2,1)S(1)}, bf16[2,8,4,32,128]{4,3,2,1,0:T(8,128)(2,1)S(1)}, u32[]{:S(2)}, u32[]{:S(2)}) %collective-permute-start.6) | collective-permute-done | bytes 524320 | tf_op jit(solution)/shard_map/ppermute | solution.py:21
  139.8 4.1 %collective-permute-done.11.refs_7_ = bf16[2,8,4,32,128]{4,3,2,1,0:T(8,128)(2,1)} collective-permute-done((bf16[2,8,4,32,128]{4,3,2,1,0:T(8,128)(2,1)S(1)}, bf16[2,8,4,32,128]{4,3,2,1,0:T(8,128)(2,1)}, u32[]{:S(2)}, u32[]{:S(2)}) %collective-permute-start.11) | collective-permute-done | bytes 524320 | tf_op jit(solution)/shard_map/ppermute | solution.py:21
  144.8 4.8 %collective-permute-done.7.refs_3_ = bf16[2,8,4,32,128]{4,3,2,1,0:T(8,128)(2,1)} collective-permute-done((bf16[2,8,4,32,128]{4,3,2,1,0:T(8,128)(2,1)S(1)}, bf16[2,8,4,32,128]{4,3,2,1,0:T(8,128)(2,1)}, u32[]{:S(2)}, u32[]{:S(2)}) %collective-permute-start.7) | collective-permute-done | bytes 524320 | tf_op jit(solution)/shard_map/ppermute | solution.py:21
  150.4 9.6 %collective-permute-done.9.refs_4_ = bf16[2,8,4,32,128]{4,3,2,1,0:T(8,128)(2,1)} collective-permute-done((bf16[2,8,4,32,128]{4,3,2,1,0:T(8,128)(2,1)S(1)}, bf16[2,8,4,32,128]{4,3,2,1,0:T(8,128)(2,1)}, u32[]{:S(2)}, u32[]{:S(2)}) %collective-permute-start.9) | collective-permute-done | bytes 524320 | tf_op jit(solution)/shard_map/ppermute | solution.py:21
  161.3 2.1 collective-permute-done.10.refs_5_
  163.6 2.2 collective-permute-done.17.refs_13_
  166.8 1.0 copy-done.3
  167.8 1.0 copy-done.5
  170.9 1.0 copy-done.11
  172.0 16.9 %ladder.1 = bf16[512,512]{1,0:T(8,128)(2,1)S(1)} custom-call(s32[3]{0:T(128)S(1)} %pad_add_fusion.where_ref, bf16[2,4,8,2,2,2,32,128]{7,6,5,4,3,2,1,0:T(8,128)(2,1)} %bitcast.6.got_hbm, bf16[2,8,4,32,128]{4,3,2,1,0:T(8,128)(2,1)S(1)} %pad_maximum_fusion.1.refs_0_, bf16[2,8,4,32,128]{4,3,2,1,0:T(8,128)(2,1)S(1)} %constant_dynamic-update-slice_fusion.refs_1_, ...), custom_call_target="tpu_custom_call" | custom-call | tf_op jit(solution)/shard_map/ladder/pallas_call | solution.py:176
  188.9 31.4 %all_to_all.10 = bf16[64,8,512]{2,1,0:T(8,128)(2,1)S(1)} all-to-all(bf16[64,8,512]{2,1,0:T(8,128)(2,1)S(1)} %bitcast.20), channel_id=1, replica_groups=mesh['yh'=2,'x'=4,'z'=8,'yl'=2,'co'=2] {'yh','x','z'}, dimensions={0} | all-to-all | bytes 1048576 | tf_op jit(solution)/shard_map/all_to_all | solution.py:235
  (65 shorter events, 12.1 us)
Async XLA Ops:
  3.9 7.5 %collective-permute-start = (bf16[1,4,32,128]{3,2,1,0:T(8,128)(2,1)S(1)}, bf16[1,4,32,128]{3,2,1,0:T(8,128)(2,1)S(1)}, u32[]{:S(2)}, u32[]{:S(2)}) collective-permute-start(bf16[1,4,32,128]{3,2,1,0:T(8,128)(2,1)S(1)} %bitcast.28), channel_id=1, source_target_pairs={{0,4},{4,0},{8,12},{12,8},{16,20},{20,16},{24,28},{28,24},{1,5},{5... | collective-permute-start | bytes 98312 | tf_op jit(solution)/shard_map/ppermute | solution.py:21
  11.4 5.6 %collective-permute-start.1 = (bf16[2,4,32,128]{3,2,1,0:T(8,128)(2,1)S(1)}, bf16[2,4,32,128]{3,2,1,0:T(8,128)(2,1)S(1)}, u32[]{:S(2)}, u32[]{:S(2)}) collective-permute-start(bf16[2,4,32,128]{3,2,1,0:T(8,128)(2,1)S(1)} %pad_maximum_fusion.4), channel_id=1, source_target_pairs={{0,8},{4,12},{8,0},{12,4},{16,24},{20,28},{24,16},{28,20},{1,9},{5... | collective-permute-start | bytes 196616 | tf_op jit(solution)/shard_map/ppermute | solution.py:21
  17.0 12.4 %collective-permute-start.2 = (bf16[4,4,32,128]{3,2,1,0:T(8,128)(2,1)S(1)}, bf16[4,4,32,128]{3,2,1,0:T(8,128)(2,1)S(1)}, u32[]{:S(2)}, u32[]{:S(2)}) collective-permute-start(bf16[4,4,32,128]{3,2,1,0:T(8,128)(2,1)S(1)} %pad_maximum_fusion.3), channel_id=1, source_target_pairs={{0,24},{4,28},{8,16},{12,20},{16,8},{20,12},{24,0},{28,4},{1,25},{... | collective-permute-start | bytes 393224 | tf_op jit(solution)/shard_map/ppermute | solution.py:21
  29.4 12.4 %copy-start.12 = (bf16[128,4,2,512]{3,2,1,0:T(2,128)(2,1)S(1)}, bf16[128,4,2,512]{3,2,1,0:T(2,128)(2,1)}, u32[]{:S(2)}) copy-start(bf16[128,4,2,512]{3,2,1,0:T(2,128)(2,1)} %param.5) | copy-start | bytes 3145732
  29.5 136.3 %all-to-all-start = ((bf16[256,64,128]{2,1,0:T(8,128)(2,1)}), bf16[256,64,128]{2,1,0:T(8,128)(2,1)}, u32[]{:S(2)}, u32[]{:S(2)}) async-start(bf16[256,64,128]{2,1,0:T(8,128)(2,1)} %bitcast.21), calls=%async_computation | async-start | bytes 8388608 | tf_op jit(solution)/shard_map/all_to_all | solution.py:216
  42.1 59.4 %collective-permute-start.20 = (bf16[1,8,128,512]{3,2,1,0:T(8,128)(2,1)S(1)}, bf16[1,8,128,512]{3,2,1,0:T(8,128)(2,1)S(1)}, u32[]{:S(2)}, u32[]{:S(2)}) collective-permute-start(bf16[1,8,128,512]{3,2,1,0:T(8,128)(2,1)S(1)} %bitcast.22), channel_id=1, source_target_pairs={{0,2},{2,0},{1,3},{3,1},{4,6},{6,4},{5,7},{7,5},{8,10},{10,8},{9,1... | collective-permute-start | bytes 3145736 | tf_op jit(solution)/shard_map/ppermute | solution.py:21
  42.2 56.1 %collective-permute-start.3 = (bf16[1,8,4,32,128]{4,3,2,1,0:T(8,128)(2,1)S(1)}, bf16[1,8,4,32,128]{4,3,2,1,0:T(8,128)(2,1)S(1)}, u32[]{:S(2)}, u32[]{:S(2)}) collective-permute-start(bf16[1,8,4,32,128]{4,3,2,1,0:T(8,128)(2,1)S(1)} %bitcast.24), channel_id=1, source_target_pairs={{0,2},{2,0},{128,130},{130,128},{1,3},{3,1},{129,131},{131,129},{4... | collective-permute-start | bytes 786440 | tf_op jit(solution)/shard_map/ppermute | solution.py:21
  98.3 29.4 %collective-permute-start.12 = (bf16[2,8,4,32,128]{4,3,2,1,0:T(8,128)(2,1)S(1)}, bf16[2,8,4,32,128]{4,3,2,1,0:T(8,128)(2,1)S(1)}, u32[]{:S(2)}, u32[]{:S(2)}) collective-permute-start(bf16[2,8,4,32,128]{4,3,2,1,0:T(8,128)(2,1)S(1)} %pad_maximum_fusion.1.refs_0_), channel_id=1, source_target_pairs={{0,1},{1,0},{2,3},{3,2},{4,5},{5,4},{6,7},{7,6},{8,9},{9,8},{10,11... | collective-permute-start | bytes 1572872 | tf_op jit(solution)/shard_map/ppermute | solution.py:21
  98.4 30.1 %collective-permute-start.8 = (bf16[2,8,4,32,128]{4,3,2,1,0:T(8,128)(2,1)S(1)}, bf16[2,8,4,32,128]{4,3,2,1,0:T(8,128)(2,1)S(1)}, u32[]{:S(2)}, u32[]{:S(2)}) collective-permute-start(bf16[2,8,4,32,128]{4,3,2,1,0:T(8,128)(2,1)S(1)} %pad_maximum_fusion.1.refs_0_), channel_id=1, source_target_pairs={{0,96},{32,64},{64,32},{96,0},{1,97},{33,65},{65,33},{97,1},{2,98}... | collective-permute-start | bytes 1572872 | tf_op jit(solution)/shard_map/ppermute | solution.py:21
  101.7 64.0 %collective-permute-start.21 = (bf16[2,8,128,512]{3,2,1,0:T(8,128)(2,1)S(1)}, bf16[2,8,128,512]{3,2,1,0:T(8,128)(2,1)}, u32[]{:S(2)}, u32[]{:S(2)}) collective-permute-start(bf16[2,8,128,512]{3,2,1,0:T(8,128)(2,1)S(1)} %pad_maximum_fusion.refs_16_), channel_id=1, source_target_pairs={{0,1},{1,0},{2,3},{3,2},{4,5},{5,4},{6,7},{7,6},{8,9},{9,8},{10,11... | collective-permute-start | bytes 6291464 | tf_op jit(solution)/shard_map/ppermute | solution.py:21
  101.8 15.4 %collective-permute-start.4 = (bf16[1,8,4,32,128]{4,3,2,1,0:T(8,128)(2,1)S(1)}, bf16[1,8,4,32,128]{4,3,2,1,0:T(8,128)(2,1)S(1)}, u32[]{:S(2)}, u32[]{:S(2)}) collective-permute-start(bf16[1,8,4,32,128]{4,3,2,1,0:T(8,128)(2,1)S(1)} %bitcast.26), channel_id=1, source_target_pairs={{0,128},{2,130},{128,0},{130,2},{1,129},{3,131},{129,1},{131,3},{4... | collective-permute-start | bytes 786440 | tf_op jit(solution)/shard_map/ppermute | solution.py:21
  104.6 22.6 %collective-permute-start.5 = (bf16[1,8,4,32,128]{4,3,2,1,0:T(8,128)(2,1)S(1)}, bf16[1,8,4,32,128]{4,3,2,1,0:T(8,128)(2,1)S(1)}, u32[]{:S(2)}, u32[]{:S(2)}) collective-permute-start(bf16[1,8,4,32,128]{4,3,2,1,0:T(8,128)(2,1)S(1)} %bitcast.27), channel_id=1, source_target_pairs={{0,130},{2,128},{128,2},{130,0},{1,131},{3,129},{129,3},{131,1},{4... | collective-permute-start | bytes 786440 | tf_op jit(solution)/shard_map/ppermute | solution.py:21
  117.2 21.1 %collective-permute-start.6 = (bf16[2,8,4,32,128]{4,3,2,1,0:T(8,128)(2,1)S(1)}, bf16[2,8,4,32,128]{4,3,2,1,0:T(8,128)(2,1)S(1)}, u32[]{:S(2)}, u32[]{:S(2)}) collective-permute-start(bf16[2,8,4,32,128]{4,3,2,1,0:T(8,128)(2,1)S(1)} %pad_maximum_fusion.1.refs_0_), channel_id=1, source_target_pairs={{0,32},{32,0},{64,96},{96,64},{1,33},{33,1},{65,97},{97,65},{2,34}... | collective-permute-start | bytes 1572872 | tf_op jit(solution)/shard_map/ppermute | solution.py:21
  127.2 11.0 %collective-permute-start.13 = (bf16[2,8,4,32,128]{4,3,2,1,0:T(8,128)(2,1)S(1)}, bf16[2,8,4,32,128]{4,3,2,1,0:T(8,128)(2,1)S(1)}, u32[]{:S(2)}, u32[]{:S(2)}) collective-permute-start(bf16[2,8,4,32,128]{4,3,2,1,0:T(8,128)(2,1)S(1)} %constant_dynamic-update-slice_fusion.refs_1_), channel_id=1, source_target_pairs={{0,1},{1,0},{2,3},{3,2},{4,5},{5,4},{6,7},{7,6},{8,9},{9,8},{10,11... | collective-permute-start | bytes 1572872 | tf_op jit(solution)/shard_map/ppermute | solution.py:21
  128.6 15.4 %collective-permute-start.11 = (bf16[2,8,4,32,128]{4,3,2,1,0:T(8,128)(2,1)S(1)}, bf16[2,8,4,32,128]{4,3,2,1,0:T(8,128)(2,1)}, u32[]{:S(2)}, u32[]{:S(2)}) collective-permute-start(bf16[2,8,4,32,128]{4,3,2,1,0:T(8,128)(2,1)S(1)} %constant_dynamic-update-slice_fusion.refs_1_), channel_id=1, source_target_pairs={{0,96},{32,64},{64,32},{96,0},{1,97},{33,65},{65,33},{97,1},{2,98}... | collective-permute-start | bytes 1572872 | tf_op jit(solution)/shard_map/ppermute | solution.py:21
  128.6 21.0 %collective-permute-start.7 = (bf16[2,8,4,32,128]{4,3,2,1,0:T(8,128)(2,1)S(1)}, bf16[2,8,4,32,128]{4,3,2,1,0:T(8,128)(2,1)}, u32[]{:S(2)}, u32[]{:S(2)}) collective-permute-start(bf16[2,8,4,32,128]{4,3,2,1,0:T(8,128)(2,1)S(1)} %constant_dynamic-update-slice_fusion.refs_1_), channel_id=1, source_target_pairs={{0,32},{32,0},{64,96},{96,64},{1,33},{33,1},{65,97},{97,65},{2,34}... | collective-permute-start | bytes 1572872 | tf_op jit(solution)/shard_map/ppermute | solution.py:21
  138.3 11.3 %collective-permute-start.18 = (bf16[2,8,4,32,128]{4,3,2,1,0:T(8,128)(2,1)S(1)}, bf16[2,8,4,32,128]{4,3,2,1,0:T(8,128)(2,1)S(1)}, u32[]{:S(2)}, u32[]{:S(2)}) collective-permute-start(bf16[2,8,4,32,128]{4,3,2,1,0:T(8,128)(2,1)S(1)} %collective-permute-done.8.refs_6_), channel_id=1, source_target_pairs={{0,1},{1,0},{2,3},{3,2},{4,5},{5,4},{6,7},{7,6},{8,9},{9,8},{10,11... | collective-permute-start | bytes 1572872 | tf_op jit(solution)/shard_map/ppermute | solution.py:21
  139.0 21.0 %collective-permute-start.9 = (bf16[2,8,4,32,128]{4,3,2,1,0:T(8,128)(2,1)S(1)}, bf16[2,8,4,32,128]{4,3,2,1,0:T(8,128)(2,1)}, u32[]{:S(2)}, u32[]{:S(2)}) collective-permute-start(bf16[2,8,4,32,128]{4,3,2,1,0:T(8,128)(2,1)S(1)} %collective-permute-done.8.refs_6_), channel_id=1, source_target_pairs={{0,32},{32,0},{64,96},{96,64},{1,33},{33,1},{65,97},{97,65},{2,34}... | collective-permute-start | bytes 1572872 | tf_op jit(solution)/shard_map/ppermute | solution.py:21
  144.0 16.1 %collective-permute-start.14 = (bf16[2,8,4,32,128]{4,3,2,1,0:T(8,128)(2,1)S(1)}, bf16[2,8,4,32,128]{4,3,2,1,0:T(8,128)(2,1)S(1)}, u32[]{:S(2)}, u32[]{:S(2)}) collective-permute-start(bf16[2,8,4,32,128]{4,3,2,1,0:T(8,128)(2,1)S(1)} %collective-permute-done.6.refs_2_), channel_id=1, source_target_pairs={{0,1},{1,0},{2,3},{3,2},{4,5},{5,4},{6,7},{7,6},{8,9},{9,8},{10,11... | collective-permute-start | bytes 1572872 | tf_op jit(solution)/shard_map/ppermute | solution.py:21
  149.6 13.9 %collective-permute-start.10 = (bf16[2,8,4,32,128]{4,3,2,1,0:T(8,128)(2,1)}, bf16[2,8,4,32,128]{4,3,2,1,0:T(8,128)(2,1)}, u32[]{:S(2)}, u32[]{:S(2)}) collective-permute-start(bf16[2,8,4,32,128]{4,3,2,1,0:T(8,128)(2,1)} %collective-permute-done.7.refs_3_), channel_id=1, source_target_pairs={{0,96},{32,64},{64,32},{96,0},{1,97},{33,65},{65,33},{97,1},{2,98}... | collective-permute-start | bytes 1572872 | tf_op jit(solution)/shard_map/ppermute | solution.py:21
  150.4 13.1 %collective-permute-start.15 = (bf16[2,8,4,32,128]{4,3,2,1,0:T(8,128)(2,1)}, bf16[2,8,4,32,128]{4,3,2,1,0:T(8,128)(2,1)}, u32[]{:S(2)}, u32[]{:S(2)}) collective-permute-start(bf16[2,8,4,32,128]{4,3,2,1,0:T(8,128)(2,1)} %collective-permute-done.7.refs_3_), channel_id=1, source_target_pairs={{0,1},{1,0},{2,3},{3,2},{4,5},{5,4},{6,7},{7,6},{8,9},{9,8},{10,11... | collective-permute-start | bytes 1572872 | tf_op jit(solution)/shard_map/ppermute | solution.py:21
  160.0 3.5 %collective-permute-start.19 = (bf16[2,8,4,32,128]{4,3,2,1,0:T(8,128)(2,1)}, bf16[2,8,4,32,128]{4,3,2,1,0:T(8,128)(2,1)}, u32[]{:S(2)}, u32[]{:S(2)}) collective-permute-start(bf16[2,8,4,32,128]{4,3,2,1,0:T(8,128)(2,1)} %collective-permute-done.11.refs_7_), channel_id=1, source_target_pairs={{0,1},{1,0},{2,3},{3,2},{4,5},{5,4},{6,7},{7,6},{8,9},{9,8},{10,11... | collective-permute-start | bytes 1572872 | tf_op jit(solution)/shard_map/ppermute | solution.py:21
  160.8 2.7 %collective-permute-start.16 = (bf16[2,8,4,32,128]{4,3,2,1,0:T(8,128)(2,1)}, bf16[2,8,4,32,128]{4,3,2,1,0:T(8,128)(2,1)}, u32[]{:S(2)}, u32[]{:S(2)}) collective-permute-start(bf16[2,8,4,32,128]{4,3,2,1,0:T(8,128)(2,1)} %collective-permute-done.9.refs_4_), channel_id=1, source_target_pairs={{0,1},{1,0},{2,3},{3,2},{4,5},{5,4},{6,7},{7,6},{8,9},{9,8},{10,11... | collective-permute-start | bytes 1572872 | tf_op jit(solution)/shard_map/ppermute | solution.py:21
  163.5 2.3 %collective-permute-start.17 = (bf16[2,8,4,32,128]{4,3,2,1,0:T(8,128)(2,1)}, bf16[2,8,4,32,128]{4,3,2,1,0:T(8,128)(2,1)}, u32[]{:S(2)}, u32[]{:S(2)}) collective-permute-start(bf16[2,8,4,32,128]{4,3,2,1,0:T(8,128)(2,1)} %collective-permute-done.10.refs_5_), channel_id=1, source_target_pairs={{0,1},{1,0},{2,3},{3,2},{4,5},{5,4},{6,7},{7,6},{8,9},{9,8},{10,11... | collective-permute-start | bytes 1572872 | tf_op jit(solution)/shard_map/ppermute | solution.py:21
  (12 other events, 11.1 us)
